TPU v7x, 32 devices: a whole 2x2x4 slice. The times are simulated.
32 devices in a mesh: row: 8 (over y, x, core), col: 4 (over z).
Axes of the slice: x: 2, y: 2, z: 4, core: 2. Of those that a mesh axis runs over, the one named last changes fastest.
Arguments:
- spectra: float32 [2, 3, 8, 512, 1024], P(None, None, 'row', 'col'), may hold values from -6 to 6
- history: bfloat16 [16, 3, 8, 128, 128], P(None, None, 'row', 'col'), as said below
- steps: int32 [16], replicated, may hold values from 0 to 15, each once
- basis: bfloat16 [256, 3, 8, 128, 128], P(None, None, 'row', 'col'), as said below
Outputs:
- velocity: float32 [3, 8, 1024, 1024], P(None, 'row', 'col')
- coeffs: float32 [256, 16], replicated
- factor: float32 [16, 16], replicated
- ortho: float32 [16, 3, 8, 128, 128], P(None, None, 'row', 'col')
Inputs may be any that keep to these rules, and one draw needn't show every extreme that they name: `steps`: each stored snapshot index appears once. `history`: every entry lies between -0.75 and 0.75. `basis`: every entry is at most 6 / sqrt(393216) in magnitude.
All inputs are finite; a program needn't handle non-finite values.
Results may differ from a plain program's by a relative error of at most 0.0012.
Values sent between devices are 32-bit elements; how exact they have to be, the bound alone decides.
No kernel may reach another device: no remote copies, remote signals or barrier semaphores. Data moves between devices by JAX's collectives and lax.ppermute only.
A program may use at most 128 MiB of HBM per device.

v0:
```python
import functools
import math

import jax
import jax.numpy as jnp
import ml_dtypes
import numpy as np
from jax import lax
from jax.experimental import pallas as pl
from jax.experimental.pallas import tpu as pltpu
from jax.sharding import PartitionSpec as P


STRIDE = 8
SNAPS = 16
RADIX = 4
LANES = 128
TAIL = 8
TILE = 16
NT = (((1,), (1,)), ((), ()))
NN = (((1,), (0,)), ((), ()))


def halves(table):
    table = table.astype(np.float32)
    high = table.astype(ml_dtypes.bfloat16)
    low = (table - high.astype(np.float32)).astype(ml_dtypes.bfloat16)
    return np.stack([high, low])


@functools.lru_cache(maxsize=None)
def tables(grid_len, mode_count, col_count, stride):
    local = mode_count // col_count
    quarter = grid_len // RADIX
    index = np.arange(quarter)
    phase = 2.0 * np.pi / quarter * (index[:, None] * index[None, :] % quarter)
    dft = halves(np.concatenate([np.cos(phase), -np.sin(phase)], axis=1))
    twiddle_phase = 2.0 * np.pi / grid_len * np.arange(RADIX)[:, None] * index[None, :]
    twiddle = np.zeros((2 * RADIX, quarter), np.float32)
    twiddle[0::2] = np.cos(twiddle_phase)
    twiddle[1::2] = np.sin(twiddle_phase)
    modes = np.arange(mode_count)
    weight = np.where(modes == 0, 1.0, 2.0)[:, None] / grid_len
    place = np.arange(grid_len)
    phase = 2.0 * np.pi / grid_len * (modes[:, None] * place[None, :] % grid_len)
    full = np.stack([weight * np.cos(phase), -weight * np.sin(phase)])
    full = full.reshape(2, col_count, local // 2, 2, grid_len).transpose(1, 3, 0, 2, 4)
    along_x = halves(full.reshape(col_count, 2, local, grid_len)[..., : grid_len // 2])
    mean = full.reshape(col_count, 2 * local, grid_len // stride, stride).sum(-1) / stride**2
    return dft, twiddle, along_x, halves(mean)


def in_hbm(array):
    return pltpu.with_memory_space_constraint(array, pltpu.HBM)


def in_vmem(array):
    return pltpu.with_memory_space_constraint(array, pltpu.VMEM)


def split(value):
    high = value.astype(jnp.bfloat16)
    return high, (value - high.astype(jnp.float32)).astype(jnp.bfloat16)


def product(left, right, dims):
    dot = functools.partial(
        lax.dot_general, dimension_numbers=dims, preferred_element_type=jnp.float32
    )
    return dot(left[0], right[0]) + (dot(left[0], right[1]) + dot(left[1], right[0]))


def wave_kernel(first, count, final, plan, col_ref, spec_hbm, dft_hbm, twiddle_hbm, mean_hbm, *refs):
    spec_ref, dft_ref, twiddle_ref, mean_ref, sum_ref, lane_ref, sems = refs[-7:]
    others, refs = refs[: first if final else 0], refs[first if final else 0 : -7]
    local, grid_len = spec_ref.shape[-2:]
    quarter = grid_len // RADIX
    col_count = 1 + max(shift for _, shift, _, _ in plan)
    out_refs, part_refs = refs[: len(plan)], refs[len(plan) :]
    block = quarter // col_count
    col = col_ref[0]
    copies = []
    for b in range(count):
        copies.append(
            pltpu.make_async_copy(spec_hbm.at[:, first + b, 0], spec_ref.at[b], sems.at[b])
        )
    copies.append(pltpu.make_async_copy(dft_hbm, dft_ref, sems.at[count]))
    copies.append(pltpu.make_async_copy(mean_hbm.at[:, col], mean_ref, sems.at[count + 1]))
    copies.append(pltpu.make_async_copy(twiddle_hbm, twiddle_ref, sems.at[count + 2]))
    for copy in copies:
        copy.start()
    starts = [
        pl.multiple_of(lax.rem(col + shift, col_count) * block, block) for shift in range(col_count)
    ]
    for b in range(count):
        copies[b].wait()
        for part in range(2):
            for lane in range(grid_len // LANES):
                lane_ref[part, lane] = spec_ref[b, part, :, lane * LANES : (lane + 1) * LANES]
        if b == 0:
            copies[count].wait()
            copies[count + 2].wait()
        dft = [
            jnp.concatenate([dft_ref[half, pl.ds(start, block), :] for start in starts], axis=0)
            for half in range(2)
        ]

        def piece(parity, part, r):
            per = quarter // LANES
            rows = pl.ds(parity, local // 2, stride=2)
            return jnp.concatenate(
                [lane_ref[part, lane, rows, :] for lane in range(r * per, (r + 1) * per)], axis=1
            )

        even_odd = {}
        for parity in range(2):
            for part in range(2):
                s0, s1, s2, s3 = [piece(parity, part, r) for r in range(RADIX)]
                even_odd[parity, part] = (s0 + s2, s1 + s3, s0 - s2, s1 - s3)
        for t in range(RADIX):
            cosine, sine = twiddle_ref[2 * t : 2 * t + 1, :], twiddle_ref[2 * t + 1 : 2 * t + 2, :]
            first_half, second_half = [], []
            for parity in range(2):
                re, im = even_odd[parity, 0], even_odd[parity, 1]
                if t == 0:
                    u_re, u_im = re[0] + re[1], im[0] + im[1]
                elif t == 2:
                    u_re, u_im = re[0] - re[1], im[0] - im[1]
                elif t == 1:
                    u_re, u_im = re[2] - im[3], im[2] + re[3]
                else:
                    u_re, u_im = re[2] + im[3], im[2] - re[3]
                if t == 0:
                    v_re, v_im = u_re, u_im
                else:
                    v_re = u_re * cosine - u_im * sine
                    v_im = u_re * sine + u_im * cosine
                first_half += [v_re, v_im]
                second_half += [v_im, -v_re]
            rows = jnp.concatenate(
                [jnp.concatenate(first_half, axis=0), jnp.concatenate(second_half, axis=0)], axis=1
            )
            wave = product(dft, split(rows), NT)
            for out_ref, (at, shift, n, size) in zip(out_refs, plan):
                if at == b:
                    start = shift * block + n * size
                    out_ref[t * size : (t + 1) * size, :] = wave[start : start + size]
            for lane in range(2 * local // LANES):
                some = wave[:, lane * LANES : (lane + 1) * LANES]
                sum_ref[lane] = some if t == 0 else sum_ref[lane] + some
        if b == 0:
            copies[count + 1].wait()
        pair = STRIDE // RADIX
        total = []
        for lane in range(2 * local // LANES):
            steps = [sum_ref[lane, pl.ds(n, quarter // pair, stride=pair), :] for n in range(pair)]
            total.append(functools.reduce(jnp.add, steps))
        total = jnp.concatenate(total, axis=1)
        mean = product(split(total), (mean_ref[0], mean_ref[1]), NN)
        if final:
            per = mean.shape[0] // col_count
            for shift in range(col_count):
                part_refs[shift][first + b] = mean[shift * per : (shift + 1) * per]
        else:
            part_refs[b][...] = mean
    for at, other in enumerate(others):
        per = other.shape[0] // col_count
        for shift in range(col_count):
            part_refs[shift][at] = other[shift * per : (shift + 1) * per]


def transform_y(col, spectra, consts, others, first, count, col_count, final):
    dft, twiddle, _, mean = consts
    components, (local, grid_len) = spectra.shape[1], spectra.shape[-2:]
    quarter = grid_len // RADIX
    rows = grid_len // col_count
    cells = grid_len // STRIDE
    vmem, hbm = pl.BlockSpec(memory_space=pltpu.VMEM), pl.BlockSpec(memory_space=pltpu.HBM)
    smem = pl.BlockSpec(memory_space=pltpu.SMEM)
    plan, outs = [], []
    for b in range(count):
        for shift in range(col_count):
            halves_of = 2 if final and b == count - 1 else 1
            for n in range(halves_of):
                plan.append((b, shift, n, rows // RADIX // halves_of))
                tail = TAIL if halves_of == 2 and shift and n == 0 else 0
                shape = (rows // halves_of + tail, 2 * local)
                outs.append(pltpu.VMEM(shape, jnp.float32))
                if shift == 0:
                    outs[-1] = jax.ShapeDtypeStruct(shape, jnp.float32)
    if final:
        outs += [pltpu.VMEM((components, cells // col_count, cells), jnp.float32)] * col_count
    else:
        outs += [pltpu.VMEM((cells, cells), jnp.float32)] * count
    out = pl.pallas_call(
        functools.partial(wave_kernel, first, count, final, plan),
        in_specs=[smem, hbm, hbm, hbm, hbm] + [vmem] * len(others),
        out_specs=[vmem] * len(outs),
        scratch_shapes=[
            pltpu.VMEM((count, 2, local, grid_len), jnp.float32),
            pltpu.VMEM(dft.shape, jnp.bfloat16),
            pltpu.VMEM(twiddle.shape, jnp.float32),
            pltpu.VMEM((2,) + mean.shape[2:], jnp.bfloat16),
            pltpu.VMEM((2 * local // LANES, quarter, LANES), jnp.float32),
            pltpu.VMEM((2, grid_len // LANES, local, LANES), jnp.float32),
            pltpu.SemaphoreType.DMA((count + 3,)),
        ],
        out_shape=outs,
        compiler_params=pltpu.CompilerParams(vmem_limit_bytes=16 << 20),
        name="transform_y",
    )(
        col,
        *[in_hbm(array) for array in (spectra, dft, twiddle, mean)],
        *[in_vmem(array) for array in others],
    )
    blocks = [[[] for _ in range(col_count)] for _ in range(count)]
    for array, (b, shift, _, _) in zip(out, plan):
        blocks[b][shift].append(array)
    return blocks, list(out[len(plan) :])


def field_kernel(component, first_row, col_count, col_ref, *refs):
    wave_refs, table_ref = refs[:col_count], refs[col_count]
    out_hbm, lane_ref, out_ref, sems = refs[-4:]
    rows, width = wave_refs[0].shape
    local = width // 2
    block = rows // RADIX
    col = col_ref[0]
    half_len = table_ref.shape[-1]
    chunk = 2 * LANES
    waves = []
    for parity in range(2):
        lanes = slice(parity * local, (parity + 1) * local)
        waves.append(split(jnp.concatenate([ref[:rows, lanes] for ref in wave_refs], axis=1)))
    sources = [lax.rem(col + col_count - shift, col_count) for shift in range(col_count)]
    copies = []
    for at in range(0, half_len, chunk):
        sums = []
        for parity in range(2):
            table = [
                jnp.concatenate(
                    [table_ref[half, source, parity, :, at : at + chunk] for source in sources],
                    axis=0,
                )
                for half in range(2)
            ]
            sums.append(product(waves[parity], table, NN))
        for side, field in enumerate((sums[0] + sums[1], sums[0] - sums[1])):
            start = side * half_len + at
            for lane in range(chunk // LANES):
                place = start // LANES + lane
                for t in range(RADIX):
                    lane_ref[place, pl.ds(t, block, stride=RADIX), :] = field[
                        t * block : (t + 1) * block, lane * LANES : (lane + 1) * LANES
                    ]
                out_ref[:, place * LANES : (place + 1) * LANES] = lane_ref[place]
            copy = pltpu.make_async_copy(
                out_ref.at[:, start : start + chunk],
                out_hbm.at[component, 0, first_row : first_row + rows, start : start + chunk],
                sems.at[len(copies)],
            )
            copy.start()
            copies.append(copy)
    for copy in copies:
        copy.wait()


def transform_x(col, waves, table, velocity, component, first_row, shape):
    rows, col_count = waves[0].shape[0], len(waves)
    in_specs = [pl.BlockSpec(memory_space=pltpu.SMEM)]
    in_specs += [pl.BlockSpec(memory_space=pltpu.VMEM)] * (col_count + 1)
    args = [col] + [in_vmem(array) for array in (*waves, table)]
    aliases = {}
    if velocity is not None:
        in_specs.append(pl.BlockSpec(memory_space=pl.ANY))
        aliases = {len(args): 0}
        args.append(velocity)
    return pl.pallas_call(
        functools.partial(field_kernel, component, first_row, col_count),
        in_specs=in_specs,
        out_specs=pl.BlockSpec(memory_space=pl.ANY),
        scratch_shapes=[
            pltpu.VMEM((shape[3] // LANES, rows, LANES), jnp.float32),
            pltpu.VMEM((rows, shape[3]), jnp.float32),
            pltpu.SemaphoreType.DMA((shape[3] // (2 * LANES),)),
        ],
        out_shape=jax.ShapeDtypeStruct(shape, jnp.float32),
        input_output_aliases=aliases,
        compiler_params=pltpu.CompilerParams(vmem_limit_bytes=16 << 20),
        name="transform_x",
    )(*args)


def project_kernel(count, steps_ref, *refs):
    part_refs, (history_ref, basis_ref, snap_ref, coeff_ref, sum_ref) = refs[:count], refs[count:]
    rank, height, cells = basis_ref.shape
    coarse = functools.reduce(jnp.add, [ref[...] for ref in part_refs])
    snap_ref[0] = coarse.reshape(height, cells).astype(jnp.bfloat16)
    for snap in range(1, SNAPS):
        snap_ref[snap] = history_ref[steps_ref[snap - 1]]

    def rows(ref, start, size):
        tiles = [
            ref[start : start + size, at : at + TILE, :].reshape(size * TILE, cells)
            for at in range(0, height, TILE)
        ]
        return jnp.concatenate(tiles, axis=1)

    right = rows(snap_ref, 0, SNAPS)
    group = 32
    shape = (group * TILE, SNAPS * TILE)
    same = lax.rem(lax.broadcasted_iota(jnp.int32, shape, 0), TILE) == lax.rem(
        lax.broadcasted_iota(jnp.int32, shape, 1), TILE
    )
    for start in range(0, rank, group):
        pairs = lax.dot_general(
            rows(basis_ref, start, group), right, NT, preferred_element_type=jnp.float32
        )
        wanted = jnp.where(same, pairs, 0.0).reshape(group, TILE, SNAPS * TILE)
        sum_ref[start : start + group, :] = jnp.sum(wanted, axis=1)
    shape = (SNAPS, SNAPS * TILE)
    fold = lax.broadcasted_iota(jnp.int32, shape, 1) // TILE == lax.broadcasted_iota(
        jnp.int32, shape, 0
    )
    coeff_ref[...] = lax.dot_general(
        jnp.where(fold, 1.0, 0.0), sum_ref[...], NT,
        precision=lax.Precision.HIGHEST, preferred_element_type=jnp.float32,
    )


def project(parts, history, steps, basis):
    vmem = pl.BlockSpec(memory_space=pltpu.VMEM)
    rank, cells = basis.shape[0], basis.shape[-1]
    basis, history = basis.reshape(rank, -1, cells), history.reshape(history.shape[0], -1, cells)
    height = basis.shape[1]
    return pl.pallas_call(
        functools.partial(project_kernel, len(parts)),
        in_specs=[pl.BlockSpec(memory_space=pltpu.SMEM)] + [vmem] * (len(parts) + 2),
        out_specs=[vmem, vmem],
        out_shape=[
            jax.ShapeDtypeStruct((SNAPS, height, cells), jnp.bfloat16),
            pltpu.VMEM((SNAPS, rank), jnp.float32),
        ],
        scratch_shapes=[pltpu.VMEM((rank, SNAPS * TILE), jnp.float32)],
        compiler_params=pltpu.CompilerParams(vmem_limit_bytes=16 << 20),
        name="project",
    )(steps, *[in_vmem(array) for array in (*parts, history, basis)])


def attach_kernel(sums_ref, *refs):
    for out_ref in refs[len(refs) // 2 :]:
        start = out_ref.shape[0] - TAIL
        for part in range(SNAPS // TAIL):
            out_ref[start:, part * LANES : part * LANES + SNAPS] = sums_ref[
                part * TAIL : (part + 1) * TAIL, :
            ]


def attach(sums, blocks):
    vmem = pl.BlockSpec(memory_space=pltpu.VMEM)
    return pl.pallas_call(
        attach_kernel,
        in_specs=[vmem] * (1 + len(blocks)),
        out_specs=[vmem] * len(blocks),
        out_shape=[pltpu.VMEM(block.shape, jnp.float32) for block in blocks],
        input_output_aliases={1 + n: n for n in range(len(blocks))},
        compiler_params=pltpu.CompilerParams(vmem_limit_bytes=16 << 20),
        name="attach",
    )(in_vmem(sums), *[in_vmem(block) for block in blocks])


def total_of(col, own_ref, block_refs, sum_ref):
    col_count = 1 + len(block_refs)
    sum_ref[col] = own_ref[...]
    for shift, block_ref in enumerate(block_refs, 1):
        source = lax.rem(col + col_count - shift, col_count)
        start = block_ref.shape[0] - TAIL
        for part in range(SNAPS // TAIL):
            sum_ref[source, part * TAIL : (part + 1) * TAIL, :] = block_ref[
                start:, part * LANES : part * LANES + SNAPS
            ]
    return functools.reduce(jnp.add, [sum_ref[source] for source in range(col_count)])


def finish_kernel(total_rows, col_count, col_ref, gram_ref, *refs):
    block_refs = refs[: col_count - 1]
    residual_ref, factor_ref, ortho_ref, sum_ref = refs[col_count - 1 :]
    gram = total_of(col_ref[0], gram_ref, block_refs, sum_ref)
    size = gram_ref.shape[0]
    row = lax.broadcasted_iota(jnp.int32, (size, size), 0)
    column = lax.broadcasted_iota(jnp.int32, (size, size), 1)
    upper = gram / total_rows
    inverse = jnp.where(row == column, 1.0, 0.0)
    for step in range(size):
        upper_row, inverse_row = upper[step : step + 1, :], inverse[step : step + 1, :]
        below = jnp.sum(jnp.where(column == step, upper, 0.0), axis=1, keepdims=True)
        pivot = below[step : step + 1, :]
        scale = 1.0 / jnp.sqrt(pivot)
        ratio = jnp.where(row > step, below / pivot, 0.0)
        upper = jnp.where(row == step, upper_row * scale, upper - ratio * upper_row)
        inverse = jnp.where(row == step, inverse_row * scale, inverse - ratio * inverse_row)
    factor_ref[...] = jnp.where(column >= row, upper, 0.0)
    ortho = jnp.dot(
        inverse, residual_ref[...], precision=lax.Precision.HIGHEST,
        preferred_element_type=jnp.float32,
    )
    cells = ortho_ref.shape[-1]
    for at in range(ortho_ref.shape[1]):
        ortho_ref[:, at, :] = ortho[:, at * cells : (at + 1) * cells]


def finish(col, gram, blocks, residual, cells, total_rows):
    vmem = pl.BlockSpec(memory_space=pltpu.VMEM)
    size, col_count = gram.shape[0], 1 + len(blocks)
    return pl.pallas_call(
        functools.partial(finish_kernel, total_rows, col_count),
        in_specs=[pl.BlockSpec(memory_space=pltpu.SMEM)] + [vmem] * (col_count + 1),
        out_specs=[vmem, vmem],
        out_shape=[
            jax.ShapeDtypeStruct((size, size), jnp.float32),
            jax.ShapeDtypeStruct((size, residual.shape[1] // cells, cells), jnp.float32),
        ],
        scratch_shapes=[pltpu.VMEM((col_count, size, size), jnp.float32)],
        compiler_params=pltpu.CompilerParams(vmem_limit_bytes=16 << 20),
        name="finish",
    )(col, gram, *[in_vmem(block) for block in blocks], residual)


def swap(value, axis, bit):
    size = lax.axis_size(axis)
    return lax.ppermute(value, axis, [(i, i ^ bit) for i in range(size)])


def sum_over(value, axis):
    bit, size = 1, lax.axis_size(axis)
    while bit < size:
        bits = (size // bit).bit_length() - 1
        if bits % 2 == 0:
            one, two, three = (swap(value, axis, bit * n) for n in (1, 2, 3))
            value = (value + one) + (two + three)
            bit *= 4
        else:
            value = value + swap(value, axis, bit)
            bit *= 2
    return value


def split_coeffs(coeffs):
    coeffs_high = coeffs.astype(jnp.bfloat16)
    high_wide = lax.optimization_barrier(coeffs_high).astype(jnp.float32)
    coeffs_low = (coeffs - high_wide).astype(jnp.bfloat16)
    return coeffs_high, lax.optimization_barrier(coeffs_low)


def residual_of(parts, snap_flat, basis):
    projected = jnp.dot(
        parts, basis.reshape(basis.shape[0], -1), preferred_element_type=jnp.float32
    )
    residual = snap_flat.astype(jnp.float32) - (projected[:SNAPS] + projected[SNAPS:])
    return residual, lax.dot_general(residual, residual, NT, precision=lax.Precision.HIGHEST)


def rows_of(residual):
    return residual.shape[1] * lax.axis_size("row") * lax.axis_size("col")


def body(spectra, history, steps, basis):
    grid_len = spectra.shape[4]
    components = spectra.shape[1]
    col_count = lax.axis_size("col")
    mode_count = spectra.shape[3] * col_count
    consts = [jnp.asarray(table) for table in tables(grid_len, mode_count, col_count, STRIDE)]
    col = lax.axis_index("col").astype(jnp.int32).reshape(1)
    groups = [(0, 1), (1, components - 1)]
    waves, parts, last = [], [], components - 1
    for first, count in groups:
        final = first + count == components
        blocks, parts = transform_y(col, spectra, consts, parts, first, count, col_count, final)
        waves += blocks

    def send(block, shift):
        perm = [(i, (i + shift) % col_count) for i in range(col_count)]
        return lax.ppermute(block, "col", perm)

    shifts = range(1, col_count)
    for shift in shifts:
        parts[shift] = send(parts[shift], shift)
        for component in range(last):
            block = waves[component][shift][0]
            waves[component][shift] = [send(block, shift)]
    snapshots, coeffs = project(parts, history, steps, basis)
    coeffs = sum_over(sum_over(coeffs, "col"), "row")
    coeff_parts = jnp.concatenate(split_coeffs(coeffs), axis=0)
    residual, gram = residual_of(coeff_parts, snapshots.reshape(SNAPS, -1), basis)
    gram = sum_over(gram, "row")
    heads = attach(gram, [waves[last][shift][0] for shift in shifts])
    for shift in shifts:
        head = send(heads[shift - 1], shift)
        waves[last][shift] = [head, send(waves[last][shift][1], shift)]
    shape = (components, 1, grid_len // col_count, grid_len)
    velocity = None

    def fill(component, velocity):
        row = 0
        for arrays in zip(*waves[component]):
            velocity = transform_x(col, arrays, consts[2], velocity, component, row, shape)
            row += arrays[0].shape[0]
        return velocity

    for component in range(last):
        velocity = fill(component, velocity)
    velocity, own_gram = lax.optimization_barrier((velocity, gram))
    factor, ortho = finish(
        col, own_gram, [waves[last][shift][0] for shift in shifts], residual, history.shape[-1],
        rows_of(residual),
    )
    for component in range(last, components):
        velocity = fill(component, velocity)
    return velocity, coeffs.T, factor, ortho.reshape(history.shape)


def body_general(spectra, history, steps, basis):
    highest = lax.Precision.HIGHEST
    grid_len = spectra.shape[4]
    col_count = lax.axis_size("col")
    mode_count = spectra.shape[3] * col_count
    index_y = jnp.arange(grid_len, dtype=jnp.int32)
    phase_y = (
        2.0
        * math.pi
        / grid_len
        * (index_y[:, None] * index_y[None, :] % grid_len).astype(jnp.float32)
    )
    cos_y = jnp.cos(phase_y)
    sin_y = jnp.sin(phase_y)
    wave_real = jnp.dot(spectra[0], cos_y, precision=highest) - jnp.dot(
        spectra[1], sin_y, precision=highest
    )
    wave_imag = jnp.dot(spectra[0], sin_y, precision=highest) + jnp.dot(
        spectra[1], cos_y, precision=highest
    )
    wave = jnp.stack([wave_real, wave_imag])
    modes_x = jnp.arange(mode_count, dtype=jnp.int32)
    phase_x = (
        2.0
        * math.pi
        / grid_len
        * (modes_x[:, None] * index_y[None, :] % grid_len).astype(jnp.float32)
    )
    weight_x = jnp.where(modes_x == 0, 1.0, 2.0).astype(jnp.float32)[:, None] / grid_len
    table_x = jnp.stack([weight_x * jnp.cos(phase_x), -weight_x * jnp.sin(phase_x)])
    velocity = lax.dot_general(
        lax.all_to_all(wave, "col", split_axis=4, concat_axis=3, tiled=True),
        table_x,
        (((0, 3), (0, 1)), ((), ())),
        precision=highest,
    )
    components, planes, local_y, _ = velocity.shape
    coarse = (
        velocity.reshape(components, planes, local_y // STRIDE, STRIDE, grid_len // STRIDE, STRIDE)
        .mean(axis=(3, 5))
        .astype(jnp.bfloat16)
    )
    chosen = jnp.take(history, steps[: SNAPS - 1], axis=0)
    snap_flat = jnp.concatenate([coarse[None], chosen], axis=0).reshape(SNAPS, -1)
    basis_flat = basis.reshape(basis.shape[0], -1)
    coeffs = lax.dot_general(snap_flat, basis_flat, NT, preferred_element_type=jnp.float32)
    coeffs = sum_over(sum_over(coeffs, "col"), "row")
    parts = jnp.concatenate(split_coeffs(coeffs), axis=0)
    residual, gram = residual_of(parts, snap_flat, basis)
    gram = sum_over(sum_over(gram, "col"), "row") / rows_of(residual)
    lower_factor = jnp.linalg.cholesky(gram)
    ortho = lax.linalg.triangular_solve(lower_factor, residual, left_side=True, lower=True)
    return velocity, coeffs.T, lower_factor.T, ortho.reshape((SNAPS,) + coarse.shape)


def solution(mesh):
    in_specs = (
        P(None, None, "row", "col", None),
        P(None, None, "row", "col", None),
        P(),
        P(None, None, "row", "col", None),
    )
    out_specs = (P(None, "row", "col", None), P(), P(), P(None, None, "row", "col", None))

    rows, cols = mesh.shape["row"], mesh.shape["col"]

    def mapped(local_body):
        return jax.shard_map(
            local_body, mesh=mesh, in_specs=in_specs, out_specs=out_specs, check_vma=False
        )

    def step(spectra, history, steps, basis):
        local = spectra.shape[3] // cols
        height = spectra.shape[1] * history.shape[3] // cols
        apart = spectra.shape[2] != rows or spectra.shape[1] < 3 or cols < 4
        if apart or local % LANES or height % TILE:
            return mapped(body_general)(spectra, history, steps, basis)

        return mapped(body)(spectra, history, steps, basis)

    return step
```

profile of v0, /device:TPU:12, one launch (start us, length us, event | category | flops | bytes accessed | tf_op | source)
XLA Modules:
  0.0 117.5 jit_solution(7576542804572281473)
XLA Ops:
  0.6 2.9 %transform_y.2 = (f32[256,256]{1,0:T(8,128)S(1)}, f32[256,256]{1,0:T(8,128)S(1)}, f32[256,256]{1,0:T(8,128)S(1)}, f32[256,256]{1,0:T(8,128)S(1)}, f32[128,128]{1,0:T(8,128)S(1)}) custom-call(s32[1]{0:T(128)} %bitcast.col_ref, f32[2,3,1,128,1024]{4,3,2,1,0:T(8,128)} %spec_hbm.3, bf16[2,256,512]{2,1,0:T(8,128)(2,1)} %constant.12.clone.dft_hbm, ...), custom_call_target="tpu_custom_call" | custom-call | tf_op jit(solution)/shard_map/transform_y/pallas_call | solution.py:195
  3.5 4.5 %transform_y.3 = (f32[256,256]{1,0:T(8,128)S(1)}, f32[256,256]{1,0:T(8,128)S(1)}, f32[256,256]{1,0:T(8,128)S(1)}, f32[256,256]{1,0:T(8,128)S(1)}, f32[128,256]{1...) custom-call(s32[1]{0:T(128)} %bitcast.col_ref, ...), custom_call_target="tpu_custom_call" | custom-call | tf_op jit(solution)/shard_map/transform_y/pallas_call | solution.py:195
  8.1 1.6 %collective-permute-start.3 = (f32[3,32,128]{2,1,0:T(8,128)S(1)}, f32[3,32,128]{2,1,0:T(8,128)S(1)}, u32[]{:S(2)}, u32[]{:S(2)}) collective-permute-start(f32[3,32,128]{2,1,0:T(8,128)S(1)} %get-tuple-element.41), channel_id=1, source_target_pairs={{0,1},{1,2},{2,3},{3,0},{4,5},{5,6},{6,7},{7,4},{8,9},{9,10},{10,1... | collective-permute-start | bytes 147464 | tf_op jit(solution)/shard_map/ppermute | solution.py:483
  10.9 1.8 %collective-permute-start.5 = (f32[3,32,128]{2,1,0:T(8,128)S(1)}, f32[3,32,128]{2,1,0:T(8,128)S(1)}, u32[]{:S(2)}, u32[]{:S(2)}) collective-permute-start(f32[3,32,128]{2,1,0:T(8,128)S(1)} %get-tuple-element.43), channel_id=1, source_target_pairs={{0,3},{1,0},{2,1},{3,2},{4,7},{5,4},{6,5},{7,6},{8,11},{9,8},{10,9... | collective-permute-start | bytes 147464 | tf_op jit(solution)/shard_map/ppermute | solution.py:483
  12.8 2.0 %collective-permute-done.4.refs_2_ = f32[3,32,128]{2,1,0:T(8,128)S(1)} collective-permute-done((f32[3,32,128]{2,1,0:T(8,128)S(1)}, f32[3,32,128]{2,1,0:T(8,128)S(1)}, u32[]{:S(2)}, u32[]{:S(2)}) %collective-permute-start.4) | collective-permute-done | bytes 49184 | tf_op jit(solution)/shard_map/ppermute | solution.py:483
  15.7 2.9 %project.1 = (bf16[16,96,128]{2,1,0:T(8,128)(2,1)S(1)}, f32[16,256]{1,0:T(8,128)S(1)}) custom-call(s32[16]{0:T(128)S(1)} %copy-done.3, f32[3,32,128]{2,1,0:T(8,128)S(1)} %get-tuple-element.40.refs_0_, f32[3,32,128]{2,1,0:T(8,128)S(1)} %collective-permute-done.3.refs_1_, f32[3,32,128]{2,1,0:T(8,128)S(1)} %collective-permute-done.4.refs_2_, ...), custom_call_target="tpu_custom_call" | custom-call | tf_op jit(solution)/shard_map/project/pallas_call | solution.py:336
  20.0 1.6 %collective-permute-start.7 = (f32[16,256]{1,0:T(8,128)S(1)}, f32[16,256]{1,0:T(8,128)S(1)}, u32[]{:S(2)}, u32[]{:S(2)}) collective-permute-start(f32[16,256]{1,0:T(8,128)S(1)} %get-tuple-element.45), channel_id=1, source_target_pairs={{0,2},{1,3},{2,0},{3,1},{4,6},{5,7},{6,4},{7,5},{8,10},{9,11},{10,... | collective-permute-start | bytes 49160 | tf_op jit(solution)/shard_map/ppermute | solution.py:431
  22.5 2.1 %collective-permute-done.7 = f32[16,256]{1,0:T(8,128)S(1)} collective-permute-done((f32[16,256]{1,0:T(8,128)S(1)}, f32[16,256]{1,0:T(8,128)S(1)}, u32[]{:S(2)}, u32[]{:S(2)}) %collective-permute-start.7) | collective-permute-done | bytes 16416 | tf_op jit(solution)/shard_map/ppermute | solution.py:431
  30.3 1.7 %collective-permute-done.11 = f32[16,256]{1,0:T(8,128)S(1)} collective-permute-done((f32[16,256]{1,0:T(8,128)S(1)}, f32[16,256]{1,0:T(8,128)S(1)}, u32[]{:S(2)}, u32[]{:S(2)}) %collective-permute-start.11) | collective-permute-done | bytes 16416 | tf_op jit(solution)/shard_map/ppermute | solution.py:431
  33.3 2.0 %fusion = f32[32,12288]{1,0:T(8,128)S(1)} fusion(bf16[32,8,96,128]{3,2,1,0:T(8,128)(2,1)S(1)} %bitcast.19, bf16[16,256]{1,0:T(8,128)(2,1)S(1)} %subtract_convert_fusion, bf16[16,256]{1,0:T(8,128)(2,1)S(1)} %get-tuple-element.68), kind=kOutput, calls=%fused_computation | convolution fusion | flops 201359360 | bytes 7880704 | tf_op jit(solution)/shard_map/dot_general | solution.py:456
  46.3 4.7 %collective-permute-start.24 = (f32[256,256]{1,0:T(8,128)S(1)}, f32[256,256]{1,0:T(8,128)S(1)}, u32[]{:S(2)}, u32[]{:S(2)}) collective-permute-start(f32[256,256]{1,0:T(8,128)S(1)} %get-tuple-element.58), channel_id=1, source_target_pairs={{0,2},{1,3},{2,0},{3,1},{4,6},{5,7},{6,4},{7,5},{8,10},{9,11},{10,... | collective-permute-start | bytes 786440 | tf_op jit(solution)/shard_map/ppermute | solution.py:483
  51.0 2.0 %collective-permute-start.20 = (f32[256,256]{1,0:T(8,128)S(1)}, f32[256,256]{1,0:T(8,128)S(1)}, u32[]{:S(2)}, u32[]{:S(2)}) collective-permute-start(f32[256,256]{1,0:T(8,128)S(1)} %get-tuple-element.53), channel_id=1, source_target_pairs={{0,1},{1,2},{2,3},{3,0},{4,5},{5,6},{6,7},{7,4},{8,9},{9,10},{10,1... | collective-permute-start | bytes 786440 | tf_op jit(solution)/shard_map/ppermute | solution.py:483
  53.0 2.6 %collective-permute-done.17.refs_1_.refs_0_ = f32[136,256]{1,0:T(8,128)S(1)} collective-permute-done((f32[136,256]{1,0:T(8,128)S(1)}, f32[136,256]{1,0:T(8,128)S(1)}, u32[]{:S(2)}, u32[]{:S(2)}) %collective-permute-start.17) | collective-permute-done | bytes 139296 | tf_op jit(solution)/shard_map/ppermute | solution.py:483
  55.6 3.5 %collective-permute-start.21 = (f32[256,256]{1,0:T(8,128)S(1)}, f32[256,256]{1,0:T(8,128)S(1)}, u32[]{:S(2)}, u32[]{:S(2)}) collective-permute-start(f32[256,256]{1,0:T(8,128)S(1)} %get-tuple-element.54), channel_id=1, source_target_pairs={{0,2},{1,3},{2,0},{3,1},{4,6},{5,7},{6,4},{7,5},{8,10},{9,11},{10,... | collective-permute-start | bytes 786440 | tf_op jit(solution)/shard_map/ppermute | solution.py:483
  59.6 10.5 %collective-permute-done.24.refs_2_ = f32[256,256]{1,0:T(8,128)S(1)} collective-permute-done((f32[256,256]{1,0:T(8,128)S(1)}, f32[256,256]{1,0:T(8,128)S(1)}, u32[]{:S(2)}, u32[]{:S(2)}) %collective-permute-start.24) | collective-permute-done | bytes 262176 | tf_op jit(solution)/shard_map/ppermute | solution.py:483
  70.1 3.9 %collective-permute-start.18 = (f32[136,256]{1,0:T(8,128)S(1)}, f32[136,256]{1,0:T(8,128)S(1)}, u32[]{:S(2)}, u32[]{:S(2)}) collective-permute-start(f32[136,256]{1,0:T(8,128)S(1)} %get-tuple-element.50), channel_id=1, source_target_pairs={{0,2},{1,3},{2,0},{3,1},{4,6},{5,7},{6,4},{7,5},{8,10},{9,11},{10,... | collective-permute-start | bytes 417800 | tf_op jit(solution)/shard_map/ppermute | solution.py:483
  74.0 12.1 %collective-permute-done.25.refs_3_ = f32[256,256]{1,0:T(8,128)S(1)} collective-permute-done((f32[256,256]{1,0:T(8,128)S(1)}, f32[256,256]{1,0:T(8,128)S(1)}, u32[]{:S(2)}, u32[]{:S(2)}) %collective-permute-start.25) | collective-permute-done | bytes 262176 | tf_op jit(solution)/shard_map/ppermute | solution.py:483
  86.1 6.4 %collective-permute-done.20.refs_1_ = f32[256,256]{1,0:T(8,128)S(1)} collective-permute-done((f32[256,256]{1,0:T(8,128)S(1)}, f32[256,256]{1,0:T(8,128)S(1)}, u32[]{:S(2)}, u32[]{:S(2)}) %collective-permute-start.20) | collective-permute-done | bytes 262176 | tf_op jit(solution)/shard_map/ppermute | solution.py:483
  92.5 2.5 %collective-permute-start = (f32[128,256]{1,0:T(8,128)S(1)}, f32[128,256]{1,0:T(8,128)S(1)}, u32[]{:S(2)}, u32[]{:S(2)}) collective-permute-start(f32[128,256]{1,0:T(8,128)S(1)} %get-tuple-element.36), channel_id=1, source_target_pairs={{0,1},{1,2},{2,3},{3,0},{4,5},{5,6},{6,7},{7,4},{8,9},{9,10},{10,1... | collective-permute-start | bytes 393224 | tf_op jit(solution)/shard_map/ppermute | solution.py:483
  95.0 7.4 %collective-permute-done.21.refs_2_ = f32[256,256]{1,0:T(8,128)S(1)} collective-permute-done((f32[256,256]{1,0:T(8,128)S(1)}, f32[256,256]{1,0:T(8,128)S(1)}, u32[]{:S(2)}, u32[]{:S(2)}) %collective-permute-start.21) | collective-permute-done | bytes 262176 | tf_op jit(solution)/shard_map/ppermute | solution.py:483
  102.4 3.4 %collective-permute-start.1 = (f32[128,256]{1,0:T(8,128)S(1)}, f32[128,256]{1,0:T(8,128)S(1)}, u32[]{:S(2)}, u32[]{:S(2)}) collective-permute-start(f32[128,256]{1,0:T(8,128)S(1)} %get-tuple-element.37), channel_id=1, source_target_pairs={{0,2},{1,3},{2,0},{3,1},{4,6},{5,7},{6,4},{7,5},{8,10},{9,11},{10,... | collective-permute-start | bytes 393224 | tf_op jit(solution)/shard_map/ppermute | solution.py:483
  105.8 2.0 %transform_x.4.refs_5_ = f32[3,1,256,1024]{3,2,1,0:T(8,128)} custom-call(s32[1]{0:T(128)} %bitcast.col_ref, f32[256,256]{1,0:T(8,128)S(1)} %get-tuple-element.56.refs_0_, f32[256,256]{1,0:T(8,128)S(1)} %collective-permute-done.23.refs_1_, f32[256,256]{1,0:T(8,128)S(1)} %collective-permute-done.24.refs_2_, f32[256,256]{1,0:T(8,128)S(1)} %collective-permute-done.25.refs_3_, ...), custom_call_target="tpu_custom_call" | custom-call | tf_op jit(solution)/shard_map/transform_x/pallas_call | solution.py:278
  107.8 2.0 %transform_x.5.refs_5_ = f32[3,1,256,1024]{3,2,1,0:T(8,128)} custom-call(s32[1]{0:T(128)} %bitcast.col_ref, f32[256,256]{1,0:T(8,128)S(1)} %get-tuple-element.52.refs_0_, f32[256,256]{1,0:T(8,128)S(1)} %collective-permute-done.20.refs_1_, f32[256,256]{1,0:T(8,128)S(1)} %collective-permute-done.21.refs_2_, ...), custom_call_target="tpu_custom_call", output_to_operand_aliasing={{}: (6, {})} | custom-call | tf_op jit(solution)/shard_map/transform_x/pallas_call | solution.py:278
  110.4 3.5 %finish.1 = (f32[16,16]{1,0:T(8,128)}, f32[16,96,128]{2,1,0:T(8,128)}) custom-call(s32[1]{0:T(128)} %bitcast.col_ref, f32[16,16]{1,0:T(8,128)S(1)} %add_add_fusion.2.sums_ref.gram_ref, f32[136,256]{1,0:T(8,128)S(1)} %collective-permute-done.17.refs_1_.refs_0_, f32[136,256]{1,0:T(8,128)S(1)} %collective-permute-done.18.refs_2_.refs_1_, ...), custom_call_target="tpu_custom_call" | custom-call | tf_op jit(solution)/shard_map/finish/pallas_call | solution.py:415
  (57 shorter events, 26.8 us)
Async XLA Ops:
  8.1 4.7 %collective-permute-start.3 = (f32[3,32,128]{2,1,0:T(8,128)S(1)}, f32[3,32,128]{2,1,0:T(8,128)S(1)}, u32[]{:S(2)}, u32[]{:S(2)}) collective-permute-start(f32[3,32,128]{2,1,0:T(8,128)S(1)} %get-tuple-element.41), channel_id=1, source_target_pairs={{0,1},{1,2},{2,3},{3,0},{4,5},{5,6},{6,7},{7,4},{8,9},{9,10},{10,1... | collective-permute-start | bytes 147464 | tf_op jit(solution)/shard_map/ppermute | solution.py:483
  9.7 5.1 %collective-permute-start.4 = (f32[3,32,128]{2,1,0:T(8,128)S(1)}, f32[3,32,128]{2,1,0:T(8,128)S(1)}, u32[]{:S(2)}, u32[]{:S(2)}) collective-permute-start(f32[3,32,128]{2,1,0:T(8,128)S(1)} %get-tuple-element.42), channel_id=1, source_target_pairs={{0,2},{1,3},{2,0},{3,1},{4,6},{5,7},{6,4},{7,5},{8,10},{9,11},{10,... | collective-permute-start | bytes 147464 | tf_op jit(solution)/shard_map/ppermute | solution.py:483
  10.9 4.7 %collective-permute-start.5 = (f32[3,32,128]{2,1,0:T(8,128)S(1)}, f32[3,32,128]{2,1,0:T(8,128)S(1)}, u32[]{:S(2)}, u32[]{:S(2)}) collective-permute-start(f32[3,32,128]{2,1,0:T(8,128)S(1)} %get-tuple-element.43), channel_id=1, source_target_pairs={{0,3},{1,0},{2,1},{3,2},{4,7},{5,4},{6,5},{7,6},{8,11},{9,8},{10,9... | collective-permute-start | bytes 147464 | tf_op jit(solution)/shard_map/ppermute | solution.py:483
  18.6 3.9 %collective-permute-start.6 = (f32[16,256]{1,0:T(8,128)S(1)}, f32[16,256]{1,0:T(8,128)S(1)}, u32[]{:S(2)}, u32[]{:S(2)}) collective-permute-start(f32[16,256]{1,0:T(8,128)S(1)} %get-tuple-element.45), channel_id=1, source_target_pairs={{0,1},{1,0},{2,3},{3,2},{4,5},{5,4},{6,7},{7,6},{8,9},{9,8},{10,11... | collective-permute-start | bytes 49160 | tf_op jit(solution)/shard_map/ppermute | solution.py:431
  20.0 4.6 %collective-permute-start.7 = (f32[16,256]{1,0:T(8,128)S(1)}, f32[16,256]{1,0:T(8,128)S(1)}, u32[]{:S(2)}, u32[]{:S(2)}) collective-permute-start(f32[16,256]{1,0:T(8,128)S(1)} %get-tuple-element.45), channel_id=1, source_target_pairs={{0,2},{1,3},{2,0},{3,1},{4,6},{5,7},{6,4},{7,5},{8,10},{9,11},{10,... | collective-permute-start | bytes 49160 | tf_op jit(solution)/shard_map/ppermute | solution.py:431
  21.6 3.7 %collective-permute-start.8 = (f32[16,256]{1,0:T(8,128)S(1)}, f32[16,256]{1,0:T(8,128)S(1)}, u32[]{:S(2)}, u32[]{:S(2)}) collective-permute-start(f32[16,256]{1,0:T(8,128)S(1)} %get-tuple-element.45), channel_id=1, source_target_pairs={{0,3},{1,2},{2,1},{3,0},{4,7},{5,6},{6,5},{7,4},{8,11},{9,10},{10,... | collective-permute-start | bytes 49160 | tf_op jit(solution)/shard_map/ppermute | solution.py:431
  26.6 3.7 %collective-permute-start.10 = (f32[16,256]{1,0:T(8,128)S(1)}, f32[16,256]{1,0:T(8,128)S(1)}, u32[]{:S(2)}, u32[]{:S(2)}) collective-permute-start(f32[16,256]{1,0:T(8,128)S(1)} %add.39), channel_id=1, source_target_pairs={{0,8},{4,12},{8,0},{12,4},{16,24},{20,28},{24,16},{28,20},{1,9},{5... | collective-permute-start | bytes 49160 | tf_op jit(solution)/shard_map/ppermute | solution.py:431
  28.1 3.9 %collective-permute-start.11 = (f32[16,256]{1,0:T(8,128)S(1)}, f32[16,256]{1,0:T(8,128)S(1)}, u32[]{:S(2)}, u32[]{:S(2)}) collective-permute-start(f32[16,256]{1,0:T(8,128)S(1)} %add.39), channel_id=1, source_target_pairs={{0,16},{4,20},{8,24},{12,28},{16,0},{20,4},{24,8},{28,12},{1,17},{... | collective-permute-start | bytes 49160 | tf_op jit(solution)/shard_map/ppermute | solution.py:431
  28.6 4.6 %collective-permute-start.12 = (f32[16,256]{1,0:T(8,128)S(1)}, f32[16,256]{1,0:T(8,128)S(1)}, u32[]{:S(2)}, u32[]{:S(2)}) collective-permute-start(f32[16,256]{1,0:T(8,128)S(1)} %add.39), channel_id=1, source_target_pairs={{0,24},{4,28},{8,16},{12,20},{16,8},{20,12},{24,0},{28,4},{1,25},{... | collective-permute-start | bytes 49160 | tf_op jit(solution)/shard_map/ppermute | solution.py:431
  38.1 5.0 %collective-permute-start.14 = (f32[16,16]{1,0:T(8,128)S(1)}, f32[16,16]{1,0:T(8,128)S(1)}, u32[]{:S(2)}, u32[]{:S(2)}) collective-permute-start(f32[16,16]{1,0:T(8,128)S(1)} %add.44), channel_id=1, source_target_pairs={{0,8},{4,12},{8,0},{12,4},{16,24},{20,28},{24,16},{28,20},{1,9},{5... | collective-permute-start | bytes 3080 | tf_op jit(solution)/shard_map/ppermute | solution.py:431
  38.7 4.5 %collective-permute-start.15 = (f32[16,16]{1,0:T(8,128)S(1)}, f32[16,16]{1,0:T(8,128)S(1)}, u32[]{:S(2)}, u32[]{:S(2)}) collective-permute-start(f32[16,16]{1,0:T(8,128)S(1)} %add.44), channel_id=1, source_target_pairs={{0,16},{4,20},{8,24},{12,28},{16,0},{20,4},{24,8},{28,12},{1,17},{... | collective-permute-start | bytes 3080 | tf_op jit(solution)/shard_map/ppermute | solution.py:431
  40.2 4.5 %collective-permute-start.16 = (f32[16,16]{1,0:T(8,128)S(1)}, f32[16,16]{1,0:T(8,128)S(1)}, u32[]{:S(2)}, u32[]{:S(2)}) collective-permute-start(f32[16,16]{1,0:T(8,128)S(1)} %add.44), channel_id=1, source_target_pairs={{0,24},{4,28},{8,16},{12,20},{16,8},{20,12},{24,0},{28,4},{1,25},{... | collective-permute-start | bytes 3080 | tf_op jit(solution)/shard_map/ppermute | solution.py:431
  41.6 17.5 %collective-permute-start.23 = (f32[256,256]{1,0:T(8,128)S(1)}, f32[256,256]{1,0:T(8,128)S(1)}, u32[]{:S(2)}, u32[]{:S(2)}) collective-permute-start(f32[256,256]{1,0:T(8,128)S(1)} %get-tuple-element.57), channel_id=1, source_target_pairs={{0,1},{1,2},{2,3},{3,0},{4,5},{5,6},{6,7},{7,4},{8,9},{9,10},{10,1... | collective-permute-start | bytes 786440 | tf_op jit(solution)/shard_map/ppermute | solution.py:483
  44.7 10.9 %collective-permute-start.17 = (f32[136,256]{1,0:T(8,128)S(1)}, f32[136,256]{1,0:T(8,128)S(1)}, u32[]{:S(2)}, u32[]{:S(2)}) collective-permute-start(f32[136,256]{1,0:T(8,128)S(1)} %get-tuple-element.49), channel_id=1, source_target_pairs={{0,1},{1,2},{2,3},{3,0},{4,5},{5,6},{6,7},{7,4},{8,9},{9,10},{10,1... | collective-permute-start | bytes 417800 | tf_op jit(solution)/shard_map/ppermute | solution.py:483
  46.3 23.8 %collective-permute-start.24 = (f32[256,256]{1,0:T(8,128)S(1)}, f32[256,256]{1,0:T(8,128)S(1)}, u32[]{:S(2)}, u32[]{:S(2)}) collective-permute-start(f32[256,256]{1,0:T(8,128)S(1)} %get-tuple-element.58), channel_id=1, source_target_pairs={{0,2},{1,3},{2,0},{3,1},{4,6},{5,7},{6,4},{7,5},{8,10},{9,11},{10,... | collective-permute-start | bytes 786440 | tf_op jit(solution)/shard_map/ppermute | solution.py:483
  51.0 35.1 %collective-permute-start.25 = (f32[256,256]{1,0:T(8,128)S(1)}, f32[256,256]{1,0:T(8,128)S(1)}, u32[]{:S(2)}, u32[]{:S(2)}) collective-permute-start(f32[256,256]{1,0:T(8,128)S(1)} %get-tuple-element.59), channel_id=1, source_target_pairs={{0,3},{1,0},{2,1},{3,2},{4,7},{5,4},{6,5},{7,6},{8,11},{9,8},{10,9... | collective-permute-start | bytes 786440 | tf_op jit(solution)/shard_map/ppermute | solution.py:483
  51.0 41.5 %collective-permute-start.20 = (f32[256,256]{1,0:T(8,128)S(1)}, f32[256,256]{1,0:T(8,128)S(1)}, u32[]{:S(2)}, u32[]{:S(2)}) collective-permute-start(f32[256,256]{1,0:T(8,128)S(1)} %get-tuple-element.53), channel_id=1, source_target_pairs={{0,1},{1,2},{2,3},{3,0},{4,5},{5,6},{6,7},{7,4},{8,9},{9,10},{10,1... | collective-permute-start | bytes 786440 | tf_op jit(solution)/shard_map/ppermute | solution.py:483
  55.6 46.8 %collective-permute-start.21 = (f32[256,256]{1,0:T(8,128)S(1)}, f32[256,256]{1,0:T(8,128)S(1)}, u32[]{:S(2)}, u32[]{:S(2)}) collective-permute-start(f32[256,256]{1,0:T(8,128)S(1)} %get-tuple-element.54), channel_id=1, source_target_pairs={{0,2},{1,3},{2,0},{3,1},{4,6},{5,7},{6,4},{7,5},{8,10},{9,11},{10,... | collective-permute-start | bytes 786440 | tf_op jit(solution)/shard_map/ppermute | solution.py:483
  59.1 46.6 %collective-permute-start.22 = (f32[256,256]{1,0:T(8,128)S(1)}, f32[256,256]{1,0:T(8,128)S(1)}, u32[]{:S(2)}, u32[]{:S(2)}) collective-permute-start(f32[256,256]{1,0:T(8,128)S(1)} %get-tuple-element.55), channel_id=1, source_target_pairs={{0,3},{1,0},{2,1},{3,2},{4,7},{5,4},{6,5},{7,6},{8,11},{9,8},{10,9... | collective-permute-start | bytes 786440 | tf_op jit(solution)/shard_map/ppermute | solution.py:483
  70.1 39.6 %collective-permute-start.18 = (f32[136,256]{1,0:T(8,128)S(1)}, f32[136,256]{1,0:T(8,128)S(1)}, u32[]{:S(2)}, u32[]{:S(2)}) collective-permute-start(f32[136,256]{1,0:T(8,128)S(1)} %get-tuple-element.50), channel_id=1, source_target_pairs={{0,2},{1,3},{2,0},{3,1},{4,6},{5,7},{6,4},{7,5},{8,10},{9,11},{10,... | collective-permute-start | bytes 417800 | tf_op jit(solution)/shard_map/ppermute | solution.py:483
  86.1 24.3 %collective-permute-start.19 = (f32[136,256]{1,0:T(8,128)S(1)}, f32[136,256]{1,0:T(8,128)S(1)}, u32[]{:S(2)}, u32[]{:S(2)}) collective-permute-start(f32[136,256]{1,0:T(8,128)S(1)} %get-tuple-element.51), channel_id=1, source_target_pairs={{0,3},{1,0},{2,1},{3,2},{4,7},{5,4},{6,5},{7,6},{8,11},{9,8},{10,9... | collective-permute-start | bytes 417800 | tf_op jit(solution)/shard_map/ppermute | solution.py:483
  92.5 22.8 %collective-permute-start = (f32[128,256]{1,0:T(8,128)S(1)}, f32[128,256]{1,0:T(8,128)S(1)}, u32[]{:S(2)}, u32[]{:S(2)}) collective-permute-start(f32[128,256]{1,0:T(8,128)S(1)} %get-tuple-element.36), channel_id=1, source_target_pairs={{0,1},{1,2},{2,3},{3,0},{4,5},{5,6},{6,7},{7,4},{8,9},{9,10},{10,1... | collective-permute-start | bytes 393224 | tf_op jit(solution)/shard_map/ppermute | solution.py:483
  102.4 12.9 %collective-permute-start.1 = (f32[128,256]{1,0:T(8,128)S(1)}, f32[128,256]{1,0:T(8,128)S(1)}, u32[]{:S(2)}, u32[]{:S(2)}) collective-permute-start(f32[128,256]{1,0:T(8,128)S(1)} %get-tuple-element.37), channel_id=1, source_target_pairs={{0,2},{1,3},{2,0},{3,1},{4,6},{5,7},{6,4},{7,5},{8,10},{9,11},{10,... | collective-permute-start | bytes 393224 | tf_op jit(solution)/shard_map/ppermute | solution.py:483
  105.8 10.2 %collective-permute-start.2 = (f32[128,256]{1,0:T(8,128)S(1)}, f32[128,256]{1,0:T(8,128)S(1)}, u32[]{:S(2)}, u32[]{:S(2)}) collective-permute-start(f32[128,256]{1,0:T(8,128)S(1)} %get-tuple-element.38), channel_id=1, source_target_pairs={{0,3},{1,0},{2,1},{3,2},{4,7},{5,4},{6,5},{7,6},{8,11},{9,8},{10,9... | collective-permute-start | bytes 393224 | tf_op jit(solution)/shard_map/ppermute | solution.py:483
  (7 other events, 114.2 us)
where the time goes:
time: 120 us; the launch traced here: 118 us
  waiting for transfers between devices  53.5 us (45%)
  starting transfers between devices  38.8 us (32%)
  Pallas kernels  20.6 us (17%)
  matrix products  3.13 us (3%)
    ppermute x15, waiting for transfers between devices, send(): return lax.ppermute(block, 'col', perm)  43.3 us
    ppermute x15, starting transfers between devices, send(): return lax.ppermute(block, 'col', perm)  28.2 us
    ppermute x11, starting transfers between devices, swap(): return lax.ppermute(value, axis, [(i, i ^ bit) for i in range(size)])  10.6 us
    ppermute x11, waiting for transfers between devices, swap(): return lax.ppermute(value, axis, [(i, i ^ bit) for i in range(size)])  10.2 us
    pallas_call x2, Pallas kernels, transform_y(): pl.pallas_call(functools.partial(wave_kernel, first, count, final, plan),...  7.41 us
    pallas_call x4, Pallas kernels, transform_x(): pl.pallas_call(functools.partial(field_kernel, component, first_row, col_...  6.71 us
    pallas_call x1, Pallas kernels, finish(): pl.pallas_call(functools.partial(finish_kernel, total_rows, col_count), i...  3.48 us
    pallas_call x1, Pallas kernels, project(): pl.pallas_call(functools.partial(project_kernel, len(parts)), in_specs=[p...  2.95 us
  transfers between devices with their start and end apart: 26, of which 18 were waited for; matrix products, arithmetic and copies ran while one was open for 0% of the time, Pallas kernels for 7%

commit v1 on v0

--- a/solution.py
+++ b/solution.py
@@ -71,35 +71,39 @@
 
 
 def wave_kernel(first, count, final, plan, col_ref, spec_hbm, dft_hbm, twiddle_hbm, mean_hbm, *refs):
-    spec_ref, dft_ref, twiddle_ref, mean_ref, sum_ref, lane_ref, sems = refs[-7:]
-    others, refs = refs[: first if final else 0], refs[first if final else 0 : -7]
-    local, grid_len = spec_ref.shape[-2:]
+    dft_ref, twiddle_ref, mean_ref, sum_ref, lane_ref, sems = refs[-6:]
+    others, refs = refs[: first if final else 0], refs[first if final else 0 : -6]
+    local, grid_len = spec_hbm.shape[-2:]
+    lanes = grid_len // LANES
     quarter = grid_len // RADIX
     col_count = 1 + max(shift for _, shift, _, _ in plan)
     out_refs, part_refs = refs[: len(plan)], refs[len(plan) :]
     block = quarter // col_count
     col = col_ref[0]
-    copies = []
-    for b in range(count):
-        copies.append(
-            pltpu.make_async_copy(spec_hbm.at[:, first + b, 0], spec_ref.at[b], sems.at[b])
-        )
-    copies.append(pltpu.make_async_copy(dft_hbm, dft_ref, sems.at[count]))
-    copies.append(pltpu.make_async_copy(mean_hbm.at[:, col], mean_ref, sems.at[count + 1]))
-    copies.append(pltpu.make_async_copy(twiddle_hbm, twiddle_ref, sems.at[count + 2]))
-    for copy in copies:
+    arrivals = [
+        [
+            pltpu.make_async_copy(
+                spec_hbm.at[:, first + b, 0, :, lane * LANES : (lane + 1) * LANES],
+                lane_ref.at[b, :, lane],
+                sems.at[b * lanes + lane],
+            )
+            for lane in range(lanes)
+        ]
+        for b in range(count)
+    ]
+    ready = [
+        pltpu.make_async_copy(dft_hbm, dft_ref, sems.at[count * lanes]),
+        pltpu.make_async_copy(twiddle_hbm, twiddle_ref, sems.at[count * lanes + 1]),
+    ]
+    mean_copy = pltpu.make_async_copy(mean_hbm.at[:, col], mean_ref, sems.at[count * lanes + 2])
+    for copy in (*arrivals[0], *ready, mean_copy, *sum(arrivals[1:], [])):
         copy.start()
     starts = [
         pl.multiple_of(lax.rem(col + shift, col_count) * block, block) for shift in range(col_count)
     ]
     for b in range(count):
-        copies[b].wait()
-        for part in range(2):
-            for lane in range(grid_len // LANES):
-                lane_ref[part, lane] = spec_ref[b, part, :, lane * LANES : (lane + 1) * LANES]
-        if b == 0:
-            copies[count].wait()
-            copies[count + 2].wait()
+        for copy in arrivals[b] + (ready if b == 0 else []):
+            copy.wait()
         dft = [
             jnp.concatenate([dft_ref[half, pl.ds(start, block), :] for start in starts], axis=0)
             for half in range(2)
@@ -109,7 +113,7 @@
             per = quarter // LANES
             rows = pl.ds(parity, local // 2, stride=2)
             return jnp.concatenate(
-                [lane_ref[part, lane, rows, :] for lane in range(r * per, (r + 1) * per)], axis=1
+                [lane_ref[b, part, lane, rows, :] for lane in range(r * per, (r + 1) * per)], axis=1
             )
 
         even_odd = {}
@@ -119,7 +123,7 @@
                 even_odd[parity, part] = (s0 + s2, s1 + s3, s0 - s2, s1 - s3)
         for t in range(RADIX):
             cosine, sine = twiddle_ref[2 * t : 2 * t + 1, :], twiddle_ref[2 * t + 1 : 2 * t + 2, :]
-            first_half, second_half = [], []
+            first_half, second_half = [[], []], [[], []]
             for parity in range(2):
                 re, im = even_odd[parity, 0], even_odd[parity, 1]
                 if t == 0:
@@ -135,12 +139,18 @@
                 else:
                     v_re = u_re * cosine - u_im * sine
                     v_im = u_re * sine + u_im * cosine
-                first_half += [v_re, v_im]
-                second_half += [v_im, -v_re]
-            rows = jnp.concatenate(
-                [jnp.concatenate(first_half, axis=0), jnp.concatenate(second_half, axis=0)], axis=1
-            )
-            wave = product(dft, split(rows), NT)
+                high_re, low_re = split(v_re)
+                high_im, low_im = split(v_im)
+                for side, (part_re, part_im) in enumerate(((high_re, high_im), (low_re, low_im))):
+                    first_half[side] += [part_re, part_im]
+                    second_half[side] += [part_im, -part_re]
+            rows = [
+                jnp.concatenate(
+                    [jnp.concatenate(one, axis=0), jnp.concatenate(two, axis=0)], axis=1
+                )
+                for one, two in zip(first_half, second_half)
+            ]
+            wave = product(dft, rows, NT)
             for out_ref, (at, shift, n, size) in zip(out_refs, plan):
                 if at == b:
                     start = shift * block + n * size
@@ -149,7 +159,7 @@
                 some = wave[:, lane * LANES : (lane + 1) * LANES]
                 sum_ref[lane] = some if t == 0 else sum_ref[lane] + some
         if b == 0:
-            copies[count + 1].wait()
+            mean_copy.wait()
         pair = STRIDE // RADIX
         total = []
         for lane in range(2 * local // LANES):
@@ -197,13 +207,12 @@
         in_specs=[smem, hbm, hbm, hbm, hbm] + [vmem] * len(others),
         out_specs=[vmem] * len(outs),
         scratch_shapes=[
-            pltpu.VMEM((count, 2, local, grid_len), jnp.float32),
             pltpu.VMEM(dft.shape, jnp.bfloat16),
             pltpu.VMEM(twiddle.shape, jnp.float32),
             pltpu.VMEM((2,) + mean.shape[2:], jnp.bfloat16),
             pltpu.VMEM((2 * local // LANES, quarter, LANES), jnp.float32),
-            pltpu.VMEM((2, grid_len // LANES, local, LANES), jnp.float32),
-            pltpu.SemaphoreType.DMA((count + 3,)),
+            pltpu.VMEM((count, 2, grid_len // LANES, local, LANES), jnp.float32),
+            pltpu.SemaphoreType.DMA((count * (grid_len // LANES) + 3,)),
         ],
         out_shape=outs,
         compiler_params=pltpu.CompilerParams(vmem_limit_bytes=16 << 20),

time: 120 us -> 120 us (level)
  no operation moved by 1% of the time
where the time goes in v1:
time: 120 us; the launch traced here: 118 us
  waiting for transfers between devices  53.6 us (45%)
  starting transfers between devices  38.6 us (32%)
  Pallas kernels  20.5 us (17%)
  matrix products  3.21 us (3%)
    ppermute x15, waiting for transfers between devices, send(): return lax.ppermute(block, 'col', perm)  43.3 us
    ppermute x15, starting transfers between devices, send(): return lax.ppermute(block, 'col', perm)  28 us
    ppermute x11, starting transfers between devices, swap(): return lax.ppermute(value, axis, [(i, i ^ bit) for i in range(size)])  10.6 us
    ppermute x11, waiting for transfers between devices, swap(): return lax.ppermute(value, axis, [(i, i ^ bit) for i in range(size)])  10.3 us
    pallas_call x2, Pallas kernels, transform_y(): pl.pallas_call(functools.partial(wave_kernel, first, count, final, plan),...  7.39 us
    pallas_call x4, Pallas kernels, transform_x(): pl.pallas_call(functools.partial(field_kernel, component, first_row, col_...  6.72 us
    pallas_call x1, Pallas kernels, finish(): pl.pallas_call(functools.partial(finish_kernel, total_rows, col_count), i...  3.47 us
    pallas_call x1, Pallas kernels, project(): pl.pallas_call(functools.partial(project_kernel, len(parts)), in_specs=[p...  2.95 us
  transfers between devices with their start and end apart: 26, of which 18 were waited for; matrix products, arithmetic and copies ran while one was open for 0% of the time, Pallas kernels for 7%

profile of v1, /device:TPU:12, one launch (start us, length us, event | category | flops | bytes accessed | tf_op | source)
XLA Modules:
  0.0 117.5 jit_solution(15277569929551284959)
XLA Ops:
  0.6 3.0 %transform_y.2 = (f32[256,256]{1,0:T(8,128)S(1)}, f32[256,256]{1,0:T(8,128)S(1)}, f32[256,256]{1,0:T(8,128)S(1)}, f32[256,256]{1,0:T(8,128)S(1)}, f32[128,128]{1,0:T(8,128)S(1)}) custom-call(s32[1]{0:T(128)} %bitcast.col_ref, f32[2,3,1,128,1024]{4,3,2,1,0:T(8,128)} %spec_hbm.3, bf16[2,256,512]{2,1,0:T(8,128)(2,1)} %constant.12.clone.dft_hbm, ...), custom_call_target="tpu_custom_call" | custom-call | tf_op jit(solution)/shard_map/transform_y/pallas_call | solution.py:205
  3.7 4.4 %transform_y.3 = (f32[256,256]{1,0:T(8,128)S(1)}, f32[256,256]{1,0:T(8,128)S(1)}, f32[256,256]{1,0:T(8,128)S(1)}, f32[256,256]{1,0:T(8,128)S(1)}, f32[128,256]{1...) custom-call(s32[1]{0:T(128)} %bitcast.col_ref, ...), custom_call_target="tpu_custom_call" | custom-call | tf_op jit(solution)/shard_map/transform_y/pallas_call | solution.py:205
  8.1 1.6 %collective-permute-start.3 = (f32[3,32,128]{2,1,0:T(8,128)S(1)}, f32[3,32,128]{2,1,0:T(8,128)S(1)}, u32[]{:S(2)}, u32[]{:S(2)}) collective-permute-start(f32[3,32,128]{2,1,0:T(8,128)S(1)} %get-tuple-element.41), channel_id=1, source_target_pairs={{0,1},{1,2},{2,3},{3,0},{4,5},{5,6},{6,7},{7,4},{8,9},{9,10},{10,1... | collective-permute-start | bytes 147464 | tf_op jit(solution)/shard_map/ppermute | solution.py:492
  10.9 1.8 %collective-permute-start.5 = (f32[3,32,128]{2,1,0:T(8,128)S(1)}, f32[3,32,128]{2,1,0:T(8,128)S(1)}, u32[]{:S(2)}, u32[]{:S(2)}) collective-permute-start(f32[3,32,128]{2,1,0:T(8,128)S(1)} %get-tuple-element.43), channel_id=1, source_target_pairs={{0,3},{1,0},{2,1},{3,2},{4,7},{5,4},{6,5},{7,6},{8,11},{9,8},{10,9... | collective-permute-start | bytes 147464 | tf_op jit(solution)/shard_map/ppermute | solution.py:492
  12.7 2.0 %collective-permute-done.4.refs_2_ = f32[3,32,128]{2,1,0:T(8,128)S(1)} collective-permute-done((f32[3,32,128]{2,1,0:T(8,128)S(1)}, f32[3,32,128]{2,1,0:T(8,128)S(1)}, u32[]{:S(2)}, u32[]{:S(2)}) %collective-permute-start.4) | collective-permute-done | bytes 49184 | tf_op jit(solution)/shard_map/ppermute | solution.py:492
  15.6 2.9 %project.1 = (bf16[16,96,128]{2,1,0:T(8,128)(2,1)S(1)}, f32[16,256]{1,0:T(8,128)S(1)}) custom-call(s32[16]{0:T(128)S(1)} %copy-done.3, f32[3,32,128]{2,1,0:T(8,128)S(1)} %get-tuple-element.40.refs_0_, f32[3,32,128]{2,1,0:T(8,128)S(1)} %collective-permute-done.3.refs_1_, f32[3,32,128]{2,1,0:T(8,128)S(1)} %collective-permute-done.4.refs_2_, ...), custom_call_target="tpu_custom_call" | custom-call | tf_op jit(solution)/shard_map/project/pallas_call | solution.py:345
  22.5 2.1 %collective-permute-done.7 = f32[16,256]{1,0:T(8,128)S(1)} collective-permute-done((f32[16,256]{1,0:T(8,128)S(1)}, f32[16,256]{1,0:T(8,128)S(1)}, u32[]{:S(2)}, u32[]{:S(2)}) %collective-permute-start.7) | collective-permute-done | bytes 16416 | tf_op jit(solution)/shard_map/ppermute | solution.py:440
  30.3 1.7 %collective-permute-done.11 = f32[16,256]{1,0:T(8,128)S(1)} collective-permute-done((f32[16,256]{1,0:T(8,128)S(1)}, f32[16,256]{1,0:T(8,128)S(1)}, u32[]{:S(2)}, u32[]{:S(2)}) %collective-permute-start.11) | collective-permute-done | bytes 16416 | tf_op jit(solution)/shard_map/ppermute | solution.py:440
  33.3 2.0 %fusion = f32[32,12288]{1,0:T(8,128)S(1)} fusion(bf16[32,8,96,128]{3,2,1,0:T(8,128)(2,1)S(1)} %bitcast.19, bf16[16,256]{1,0:T(8,128)(2,1)S(1)} %subtract_convert_fusion, bf16[16,256]{1,0:T(8,128)(2,1)S(1)} %get-tuple-element.68), kind=kOutput, calls=%fused_computation | convolution fusion | flops 201359360 | bytes 7880704 | tf_op jit(solution)/shard_map/dot_general | solution.py:465
  43.1 1.7 %collective-permute-done.16 = f32[16,16]{1,0:T(8,128)S(1)} collective-permute-done((f32[16,16]{1,0:T(8,128)S(1)}, f32[16,16]{1,0:T(8,128)S(1)}, u32[]{:S(2)}, u32[]{:S(2)}) %collective-permute-start.16) | collective-permute-done | bytes 1056 | tf_op jit(solution)/shard_map/ppermute | solution.py:440
  46.3 4.7 %collective-permute-start.24 = (f32[256,256]{1,0:T(8,128)S(1)}, f32[256,256]{1,0:T(8,128)S(1)}, u32[]{:S(2)}, u32[]{:S(2)}) collective-permute-start(f32[256,256]{1,0:T(8,128)S(1)} %get-tuple-element.58), channel_id=1, source_target_pairs={{0,2},{1,3},{2,0},{3,1},{4,6},{5,7},{6,4},{7,5},{8,10},{9,11},{10,... | collective-permute-start | bytes 786440 | tf_op jit(solution)/shard_map/ppermute | solution.py:492
  51.0 2.0 %collective-permute-start.20 = (f32[256,256]{1,0:T(8,128)S(1)}, f32[256,256]{1,0:T(8,128)S(1)}, u32[]{:S(2)}, u32[]{:S(2)}) collective-permute-start(f32[256,256]{1,0:T(8,128)S(1)} %get-tuple-element.53), channel_id=1, source_target_pairs={{0,1},{1,2},{2,3},{3,0},{4,5},{5,6},{6,7},{7,4},{8,9},{9,10},{10,1... | collective-permute-start | bytes 786440 | tf_op jit(solution)/shard_map/ppermute | solution.py:492
  53.0 2.6 %collective-permute-done.17.refs_1_.refs_0_ = f32[136,256]{1,0:T(8,128)S(1)} collective-permute-done((f32[136,256]{1,0:T(8,128)S(1)}, f32[136,256]{1,0:T(8,128)S(1)}, u32[]{:S(2)}, u32[]{:S(2)}) %collective-permute-start.17) | collective-permute-done | bytes 139296 | tf_op jit(solution)/shard_map/ppermute | solution.py:492
  55.6 3.5 %collective-permute-start.21 = (f32[256,256]{1,0:T(8,128)S(1)}, f32[256,256]{1,0:T(8,128)S(1)}, u32[]{:S(2)}, u32[]{:S(2)}) collective-permute-start(f32[256,256]{1,0:T(8,128)S(1)} %get-tuple-element.54), channel_id=1, source_target_pairs={{0,2},{1,3},{2,0},{3,1},{4,6},{5,7},{6,4},{7,5},{8,10},{9,11},{10,... | collective-permute-start | bytes 786440 | tf_op jit(solution)/shard_map/ppermute | solution.py:492
  59.6 10.5 %collective-permute-done.24.refs_2_ = f32[256,256]{1,0:T(8,128)S(1)} collective-permute-done((f32[256,256]{1,0:T(8,128)S(1)}, f32[256,256]{1,0:T(8,128)S(1)}, u32[]{:S(2)}, u32[]{:S(2)}) %collective-permute-start.24) | collective-permute-done | bytes 262176 | tf_op jit(solution)/shard_map/ppermute | solution.py:492
  70.1 3.9 %collective-permute-start.18 = (f32[136,256]{1,0:T(8,128)S(1)}, f32[136,256]{1,0:T(8,128)S(1)}, u32[]{:S(2)}, u32[]{:S(2)}) collective-permute-start(f32[136,256]{1,0:T(8,128)S(1)} %get-tuple-element.50), channel_id=1, source_target_pairs={{0,2},{1,3},{2,0},{3,1},{4,6},{5,7},{6,4},{7,5},{8,10},{9,11},{10,... | collective-permute-start | bytes 417800 | tf_op jit(solution)/shard_map/ppermute | solution.py:492
  74.0 12.1 %collective-permute-done.25.refs_3_ = f32[256,256]{1,0:T(8,128)S(1)} collective-permute-done((f32[256,256]{1,0:T(8,128)S(1)}, f32[256,256]{1,0:T(8,128)S(1)}, u32[]{:S(2)}, u32[]{:S(2)}) %collective-permute-start.25) | collective-permute-done | bytes 262176 | tf_op jit(solution)/shard_map/ppermute | solution.py:492
  86.1 6.4 %collective-permute-done.20.refs_1_ = f32[256,256]{1,0:T(8,128)S(1)} collective-permute-done((f32[256,256]{1,0:T(8,128)S(1)}, f32[256,256]{1,0:T(8,128)S(1)}, u32[]{:S(2)}, u32[]{:S(2)}) %collective-permute-start.20) | collective-permute-done | bytes 262176 | tf_op jit(solution)/shard_map/ppermute | solution.py:492
  92.5 2.5 %collective-permute-start = (f32[128,256]{1,0:T(8,128)S(1)}, f32[128,256]{1,0:T(8,128)S(1)}, u32[]{:S(2)}, u32[]{:S(2)}) collective-permute-start(f32[128,256]{1,0:T(8,128)S(1)} %get-tuple-element.36), channel_id=1, source_target_pairs={{0,1},{1,2},{2,3},{3,0},{4,5},{5,6},{6,7},{7,4},{8,9},{9,10},{10,1... | collective-permute-start | bytes 393224 | tf_op jit(solution)/shard_map/ppermute | solution.py:492
  95.0 7.4 %collective-permute-done.21.refs_2_ = f32[256,256]{1,0:T(8,128)S(1)} collective-permute-done((f32[256,256]{1,0:T(8,128)S(1)}, f32[256,256]{1,0:T(8,128)S(1)}, u32[]{:S(2)}, u32[]{:S(2)}) %collective-permute-start.21) | collective-permute-done | bytes 262176 | tf_op jit(solution)/shard_map/ppermute | solution.py:492
  102.4 3.4 %collective-permute-start.1 = (f32[128,256]{1,0:T(8,128)S(1)}, f32[128,256]{1,0:T(8,128)S(1)}, u32[]{:S(2)}, u32[]{:S(2)}) collective-permute-start(f32[128,256]{1,0:T(8,128)S(1)} %get-tuple-element.37), channel_id=1, source_target_pairs={{0,2},{1,3},{2,0},{3,1},{4,6},{5,7},{6,4},{7,5},{8,10},{9,11},{10,... | collective-permute-start | bytes 393224 | tf_op jit(solution)/shard_map/ppermute | solution.py:492
  105.8 2.0 %transform_x.4.refs_5_ = f32[3,1,256,1024]{3,2,1,0:T(8,128)} custom-call(s32[1]{0:T(128)} %bitcast.col_ref, f32[256,256]{1,0:T(8,128)S(1)} %get-tuple-element.56.refs_0_, f32[256,256]{1,0:T(8,128)S(1)} %collective-permute-done.23.refs_1_, f32[256,256]{1,0:T(8,128)S(1)} %collective-permute-done.24.refs_2_, f32[256,256]{1,0:T(8,128)S(1)} %collective-permute-done.25.refs_3_, ...), custom_call_target="tpu_custom_call" | custom-call | tf_op jit(solution)/shard_map/transform_x/pallas_call | solution.py:287
  107.8 2.0 %transform_x.5.refs_5_ = f32[3,1,256,1024]{3,2,1,0:T(8,128)} custom-call(s32[1]{0:T(128)} %bitcast.col_ref, f32[256,256]{1,0:T(8,128)S(1)} %get-tuple-element.52.refs_0_, f32[256,256]{1,0:T(8,128)S(1)} %collective-permute-done.20.refs_1_, f32[256,256]{1,0:T(8,128)S(1)} %collective-permute-done.21.refs_2_, ...), custom_call_target="tpu_custom_call", output_to_operand_aliasing={{}: (6, {})} | custom-call | tf_op jit(solution)/shard_map/transform_x/pallas_call | solution.py:287
  110.4 3.5 %finish.1 = (f32[16,16]{1,0:T(8,128)}, f32[16,96,128]{2,1,0:T(8,128)}) custom-call(s32[1]{0:T(128)} %bitcast.col_ref, f32[16,16]{1,0:T(8,128)S(1)} %add_add_fusion.2.sums_ref.gram_ref, f32[136,256]{1,0:T(8,128)S(1)} %collective-permute-done.17.refs_1_.refs_0_, f32[136,256]{1,0:T(8,128)S(1)} %collective-permute-done.18.refs_2_.refs_1_, ...), custom_call_target="tpu_custom_call" | custom-call | tf_op jit(solution)/shard_map/finish/pallas_call | solution.py:424
  (57 shorter events, 26.8 us)
Async XLA Ops:
  8.1 4.7 %collective-permute-start.3 = (f32[3,32,128]{2,1,0:T(8,128)S(1)}, f32[3,32,128]{2,1,0:T(8,128)S(1)}, u32[]{:S(2)}, u32[]{:S(2)}) collective-permute-start(f32[3,32,128]{2,1,0:T(8,128)S(1)} %get-tuple-element.41), channel_id=1, source_target_pairs={{0,1},{1,2},{2,3},{3,0},{4,5},{5,6},{6,7},{7,4},{8,9},{9,10},{10,1... | collective-permute-start | bytes 147464 | tf_op jit(solution)/shard_map/ppermute | solution.py:492
  9.7 5.1 %collective-permute-start.4 = (f32[3,32,128]{2,1,0:T(8,128)S(1)}, f32[3,32,128]{2,1,0:T(8,128)S(1)}, u32[]{:S(2)}, u32[]{:S(2)}) collective-permute-start(f32[3,32,128]{2,1,0:T(8,128)S(1)} %get-tuple-element.42), channel_id=1, source_target_pairs={{0,2},{1,3},{2,0},{3,1},{4,6},{5,7},{6,4},{7,5},{8,10},{9,11},{10,... | collective-permute-start | bytes 147464 | tf_op jit(solution)/shard_map/ppermute | solution.py:492
  10.9 4.7 %collective-permute-start.5 = (f32[3,32,128]{2,1,0:T(8,128)S(1)}, f32[3,32,128]{2,1,0:T(8,128)S(1)}, u32[]{:S(2)}, u32[]{:S(2)}) collective-permute-start(f32[3,32,128]{2,1,0:T(8,128)S(1)} %get-tuple-element.43), channel_id=1, source_target_pairs={{0,3},{1,0},{2,1},{3,2},{4,7},{5,4},{6,5},{7,6},{8,11},{9,8},{10,9... | collective-permute-start | bytes 147464 | tf_op jit(solution)/shard_map/ppermute | solution.py:492
  18.6 3.9 %collective-permute-start.6 = (f32[16,256]{1,0:T(8,128)S(1)}, f32[16,256]{1,0:T(8,128)S(1)}, u32[]{:S(2)}, u32[]{:S(2)}) collective-permute-start(f32[16,256]{1,0:T(8,128)S(1)} %get-tuple-element.45), channel_id=1, source_target_pairs={{0,1},{1,0},{2,3},{3,2},{4,5},{5,4},{6,7},{7,6},{8,9},{9,8},{10,11... | collective-permute-start | bytes 49160 | tf_op jit(solution)/shard_map/ppermute | solution.py:440
  20.0 4.6 %collective-permute-start.7 = (f32[16,256]{1,0:T(8,128)S(1)}, f32[16,256]{1,0:T(8,128)S(1)}, u32[]{:S(2)}, u32[]{:S(2)}) collective-permute-start(f32[16,256]{1,0:T(8,128)S(1)} %get-tuple-element.45), channel_id=1, source_target_pairs={{0,2},{1,3},{2,0},{3,1},{4,6},{5,7},{6,4},{7,5},{8,10},{9,11},{10,... | collective-permute-start | bytes 49160 | tf_op jit(solution)/shard_map/ppermute | solution.py:440
  21.6 3.7 %collective-permute-start.8 = (f32[16,256]{1,0:T(8,128)S(1)}, f32[16,256]{1,0:T(8,128)S(1)}, u32[]{:S(2)}, u32[]{:S(2)}) collective-permute-start(f32[16,256]{1,0:T(8,128)S(1)} %get-tuple-element.45), channel_id=1, source_target_pairs={{0,3},{1,2},{2,1},{3,0},{4,7},{5,6},{6,5},{7,4},{8,11},{9,10},{10,... | collective-permute-start | bytes 49160 | tf_op jit(solution)/shard_map/ppermute | solution.py:440
  26.6 3.7 %collective-permute-start.10 = (f32[16,256]{1,0:T(8,128)S(1)}, f32[16,256]{1,0:T(8,128)S(1)}, u32[]{:S(2)}, u32[]{:S(2)}) collective-permute-start(f32[16,256]{1,0:T(8,128)S(1)} %add.39), channel_id=1, source_target_pairs={{0,8},{4,12},{8,0},{12,4},{16,24},{20,28},{24,16},{28,20},{1,9},{5... | collective-permute-start | bytes 49160 | tf_op jit(solution)/shard_map/ppermute | solution.py:440
  28.1 3.9 %collective-permute-start.11 = (f32[16,256]{1,0:T(8,128)S(1)}, f32[16,256]{1,0:T(8,128)S(1)}, u32[]{:S(2)}, u32[]{:S(2)}) collective-permute-start(f32[16,256]{1,0:T(8,128)S(1)} %add.39), channel_id=1, source_target_pairs={{0,16},{4,20},{8,24},{12,28},{16,0},{20,4},{24,8},{28,12},{1,17},{... | collective-permute-start | bytes 49160 | tf_op jit(solution)/shard_map/ppermute | solution.py:440
  28.6 4.6 %collective-permute-start.12 = (f32[16,256]{1,0:T(8,128)S(1)}, f32[16,256]{1,0:T(8,128)S(1)}, u32[]{:S(2)}, u32[]{:S(2)}) collective-permute-start(f32[16,256]{1,0:T(8,128)S(1)} %add.39), channel_id=1, source_target_pairs={{0,24},{4,28},{8,16},{12,20},{16,8},{20,12},{24,0},{28,4},{1,25},{... | collective-permute-start | bytes 49160 | tf_op jit(solution)/shard_map/ppermute | solution.py:440
  38.2 4.9 %collective-permute-start.14 = (f32[16,16]{1,0:T(8,128)S(1)}, f32[16,16]{1,0:T(8,128)S(1)}, u32[]{:S(2)}, u32[]{:S(2)}) collective-permute-start(f32[16,16]{1,0:T(8,128)S(1)} %add.44), channel_id=1, source_target_pairs={{0,8},{4,12},{8,0},{12,4},{16,24},{20,28},{24,16},{28,20},{1,9},{5... | collective-permute-start | bytes 3080 | tf_op jit(solution)/shard_map/ppermute | solution.py:440
  38.7 4.4 %collective-permute-start.15 = (f32[16,16]{1,0:T(8,128)S(1)}, f32[16,16]{1,0:T(8,128)S(1)}, u32[]{:S(2)}, u32[]{:S(2)}) collective-permute-start(f32[16,16]{1,0:T(8,128)S(1)} %add.44), channel_id=1, source_target_pairs={{0,16},{4,20},{8,24},{12,28},{16,0},{20,4},{24,8},{28,12},{1,17},{... | collective-permute-start | bytes 3080 | tf_op jit(solution)/shard_map/ppermute | solution.py:440
  40.2 4.5 %collective-permute-start.16 = (f32[16,16]{1,0:T(8,128)S(1)}, f32[16,16]{1,0:T(8,128)S(1)}, u32[]{:S(2)}, u32[]{:S(2)}) collective-permute-start(f32[16,16]{1,0:T(8,128)S(1)} %add.44), channel_id=1, source_target_pairs={{0,24},{4,28},{8,16},{12,20},{16,8},{20,12},{24,0},{28,4},{1,25},{... | collective-permute-start | bytes 3080 | tf_op jit(solution)/shard_map/ppermute | solution.py:440
  41.7 17.5 %collective-permute-start.23 = (f32[256,256]{1,0:T(8,128)S(1)}, f32[256,256]{1,0:T(8,128)S(1)}, u32[]{:S(2)}, u32[]{:S(2)}) collective-permute-start(f32[256,256]{1,0:T(8,128)S(1)} %get-tuple-element.57), channel_id=1, source_target_pairs={{0,1},{1,2},{2,3},{3,0},{4,5},{5,6},{6,7},{7,4},{8,9},{9,10},{10,1... | collective-permute-start | bytes 786440 | tf_op jit(solution)/shard_map/ppermute | solution.py:492
  44.8 10.8 %collective-permute-start.17 = (f32[136,256]{1,0:T(8,128)S(1)}, f32[136,256]{1,0:T(8,128)S(1)}, u32[]{:S(2)}, u32[]{:S(2)}) collective-permute-start(f32[136,256]{1,0:T(8,128)S(1)} %get-tuple-element.49), channel_id=1, source_target_pairs={{0,1},{1,2},{2,3},{3,0},{4,5},{5,6},{6,7},{7,4},{8,9},{9,10},{10,1... | collective-permute-start | bytes 417800 | tf_op jit(solution)/shard_map/ppermute | solution.py:492
  46.3 23.8 %collective-permute-start.24 = (f32[256,256]{1,0:T(8,128)S(1)}, f32[256,256]{1,0:T(8,128)S(1)}, u32[]{:S(2)}, u32[]{:S(2)}) collective-permute-start(f32[256,256]{1,0:T(8,128)S(1)} %get-tuple-element.58), channel_id=1, source_target_pairs={{0,2},{1,3},{2,0},{3,1},{4,6},{5,7},{6,4},{7,5},{8,10},{9,11},{10,... | collective-permute-start | bytes 786440 | tf_op jit(solution)/shard_map/ppermute | solution.py:492
  51.0 35.1 %collective-permute-start.25 = (f32[256,256]{1,0:T(8,128)S(1)}, f32[256,256]{1,0:T(8,128)S(1)}, u32[]{:S(2)}, u32[]{:S(2)}) collective-permute-start(f32[256,256]{1,0:T(8,128)S(1)} %get-tuple-element.59), channel_id=1, source_target_pairs={{0,3},{1,0},{2,1},{3,2},{4,7},{5,4},{6,5},{7,6},{8,11},{9,8},{10,9... | collective-permute-start | bytes 786440 | tf_op jit(solution)/shard_map/ppermute | solution.py:492
  51.0 41.5 %collective-permute-start.20 = (f32[256,256]{1,0:T(8,128)S(1)}, f32[256,256]{1,0:T(8,128)S(1)}, u32[]{:S(2)}, u32[]{:S(2)}) collective-permute-start(f32[256,256]{1,0:T(8,128)S(1)} %get-tuple-element.53), channel_id=1, source_target_pairs={{0,1},{1,2},{2,3},{3,0},{4,5},{5,6},{6,7},{7,4},{8,9},{9,10},{10,1... | collective-permute-start | bytes 786440 | tf_op jit(solution)/shard_map/ppermute | solution.py:492
  55.6 46.8 %collective-permute-start.21 = (f32[256,256]{1,0:T(8,128)S(1)}, f32[256,256]{1,0:T(8,128)S(1)}, u32[]{:S(2)}, u32[]{:S(2)}) collective-permute-start(f32[256,256]{1,0:T(8,128)S(1)} %get-tuple-element.54), channel_id=1, source_target_pairs={{0,2},{1,3},{2,0},{3,1},{4,6},{5,7},{6,4},{7,5},{8,10},{9,11},{10,... | collective-permute-start | bytes 786440 | tf_op jit(solution)/shard_map/ppermute | solution.py:492
  59.1 46.6 %collective-permute-start.22 = (f32[256,256]{1,0:T(8,128)S(1)}, f32[256,256]{1,0:T(8,128)S(1)}, u32[]{:S(2)}, u32[]{:S(2)}) collective-permute-start(f32[256,256]{1,0:T(8,128)S(1)} %get-tuple-element.55), channel_id=1, source_target_pairs={{0,3},{1,0},{2,1},{3,2},{4,7},{5,4},{6,5},{7,6},{8,11},{9,8},{10,9... | collective-permute-start | bytes 786440 | tf_op jit(solution)/shard_map/ppermute | solution.py:492
  70.1 39.7 %collective-permute-start.18 = (f32[136,256]{1,0:T(8,128)S(1)}, f32[136,256]{1,0:T(8,128)S(1)}, u32[]{:S(2)}, u32[]{:S(2)}) collective-permute-start(f32[136,256]{1,0:T(8,128)S(1)} %get-tuple-element.50), channel_id=1, source_target_pairs={{0,2},{1,3},{2,0},{3,1},{4,6},{5,7},{6,4},{7,5},{8,10},{9,11},{10,... | collective-permute-start | bytes 417800 | tf_op jit(solution)/shard_map/ppermute | solution.py:492
  86.1 24.3 %collective-permute-start.19 = (f32[136,256]{1,0:T(8,128)S(1)}, f32[136,256]{1,0:T(8,128)S(1)}, u32[]{:S(2)}, u32[]{:S(2)}) collective-permute-start(f32[136,256]{1,0:T(8,128)S(1)} %get-tuple-element.51), channel_id=1, source_target_pairs={{0,3},{1,0},{2,1},{3,2},{4,7},{5,4},{6,5},{7,6},{8,11},{9,8},{10,9... | collective-permute-start | bytes 417800 | tf_op jit(solution)/shard_map/ppermute | solution.py:492
  92.5 22.8 %collective-permute-start = (f32[128,256]{1,0:T(8,128)S(1)}, f32[128,256]{1,0:T(8,128)S(1)}, u32[]{:S(2)}, u32[]{:S(2)}) collective-permute-start(f32[128,256]{1,0:T(8,128)S(1)} %get-tuple-element.36), channel_id=1, source_target_pairs={{0,1},{1,2},{2,3},{3,0},{4,5},{5,6},{6,7},{7,4},{8,9},{9,10},{10,1... | collective-permute-start | bytes 393224 | tf_op jit(solution)/shard_map/ppermute | solution.py:492
  102.4 12.9 %collective-permute-start.1 = (f32[128,256]{1,0:T(8,128)S(1)}, f32[128,256]{1,0:T(8,128)S(1)}, u32[]{:S(2)}, u32[]{:S(2)}) collective-permute-start(f32[128,256]{1,0:T(8,128)S(1)} %get-tuple-element.37), channel_id=1, source_target_pairs={{0,2},{1,3},{2,0},{3,1},{4,6},{5,7},{6,4},{7,5},{8,10},{9,11},{10,... | collective-permute-start | bytes 393224 | tf_op jit(solution)/shard_map/ppermute | solution.py:492
  105.8 10.2 %collective-permute-start.2 = (f32[128,256]{1,0:T(8,128)S(1)}, f32[128,256]{1,0:T(8,128)S(1)}, u32[]{:S(2)}, u32[]{:S(2)}) collective-permute-start(f32[128,256]{1,0:T(8,128)S(1)} %get-tuple-element.38), channel_id=1, source_target_pairs={{0,3},{1,0},{2,1},{3,2},{4,7},{5,4},{6,5},{7,6},{8,11},{9,8},{10,9... | collective-permute-start | bytes 393224 | tf_op jit(solution)/shard_map/ppermute | solution.py:492
  (7 other events, 113.9 us)
